TPU v7x, 256 devices: a whole 4x4x8 slice. The times are simulated.
256 devices in a mesh: mom: 4 (over x_hi, core), en: 64 (over y, z, x_lo).
Axes of the slice: x: 4 (x_hi: 2, x_lo: 2; x = x_hi * 2 + x_lo), y: 4, z: 8, core: 2. Of those that a mesh axis runs over, the one named last changes fastest.
Arguments:
- green_less: bfloat16 [8, 1536, 8, 288], P('mom', 'en'), may hold values from -6 to 6
- green_greater: bfloat16 [8, 1536, 8, 288], P('mom', 'en'), may hold values from -6 to 6
- derivative: float32 [2, 3, 144], replicated, may hold values from -1.75 to 1.75
- neighbours: int32 [2, 4], replicated, may hold values from 0 to 1
- phonon: bfloat16 [2, 8, 24, 3, 8], replicated, may hold values from 0.0099487305 to 0.099609375
Outputs:
- self_energy: bfloat16 [8, 1536, 8, 288], P('mom', 'en')
- polarisation: float32 [8, 24, 3, 8], P('mom')
All inputs are finite; a program needn't handle non-finite values.
Results may differ from a plain program's by a relative error of at most 0.0034.
Values may be sent and summed in bfloat16 or wider, within the bound.
A program may use at most 64 MiB of HBM per device.

v0:
```python
import functools

import jax
import jax.numpy as jnp
import numpy as np
from jax import lax
from jax.experimental import pallas as pl
from jax.experimental.pallas import tpu as pltpu
from jax.sharding import PartitionSpec as P

NO = 12
NB = 4
NN = NO * NO
MESH = pl.DeviceIdType.MESH
BF = jnp.bfloat16
F32 = jnp.float32


def tables(momenta, window):
    r = np.arange(NN)
    col = np.arange(2 * NN)
    sub = col % NN
    rows_s = (r[None, :] % NO == r[:, None] // NO).astype(np.float32)
    rows_t = (r[None, :] % NO == r[:, None] % NO).astype(np.float32)
    cols_i = (r[:, None] // NO == sub[None, :] // NO).astype(np.float32)
    cols_u = (r[:, None] // NO == sub[None, :] % NO).astype(np.float32)
    flipped = (col // NN) * NN + (sub % NO) * NO + sub // NO
    swap = np.zeros((2 * NN, 2 * NN), np.float32)
    swap[flipped, col] = np.where(col < NN, 1.0, -1.0)
    place = np.zeros((2, momenta, window, 5, 32 * momenta), np.float32)
    for block in range(momenta):
        q = (-block) % momenta
        for de in range(window):
            at = 32 * block + de
            place[0, q, window - 1 - de, 0, at] = 1.0
            if de >= 1:
                place[1, q, de - 1, 1, at] = 1.0
            if de == 0:
                place[1, q, window - 1, 3, at] = 1.0
        for de in range(1 - window, 0):
            at = (32 * block + de) % (32 * momenta)
            place[0, q, -de - 1, 2, at] = 1.0
            place[1, q, window - 1 + de, 4, at] = 1.0
    place = place.reshape(2 * momenta * window, 5 * 32 * momenta)
    return rows_s, rows_t, cols_i, cols_u, swap, place


def kernel(
    dims,
    gl_ref, gg_ref, der_ref, nb_ref, coef_ref, rs_ref, rt_ref, ci_ref, cu_ref, swap_ref,
    se_ref, pol_ref,
    rows_f, gl_t, gg_t, gl, gg, toe, kr_hi, kr_lo, wgt, acc, se_t, se_r, part, got_z, plane, got_p,
    s_gg, r_gg, s_gl, r_gl, s_se, r_se, s_z, r_z, s_p, r_p,
):
    moms, ens, ny, nz, nx, own_k, own_e, pairs, momenta = dims
    pp_n = pairs // moms
    rows = own_k * own_e
    all_rows = momenta * own_e
    me = lax.axis_index("mom")
    en = lax.axis_index("en")
    iy, iz, ix = en // (nz * nx), (en // nx) % nz, en % nx
    up, down = lax.rem(en + 1, ens), lax.rem(en + ens - 1, ens)

    gl[:, :, :, own_e:, :] = jnp.zeros((3, pp_n, momenta, 32 - own_e, 2 * NN), BF)

    barrier = pltpu.get_barrier_semaphore()

    def greet(mom_at, en_at):
        pl.semaphore_signal(
            barrier, inc=1, device_id={"mom": mom_at, "en": en_at}, device_id_type=MESH
        )

    for rel in range(1, moms):
        greet(lax.rem(me + rel, moms), en)
    for rel in range(moms):
        greet(lax.rem(me + rel, moms), up)
        greet(lax.rem(me + rel, moms), down)
    for rel in range(1, nz):
        greet(me, (iy * nz + lax.rem(iz + rel, nz)) * nx + ix)
    plane_n = ny * nx * moms

    def plane_peer(rel):
        ry, rx, rm = rel // (nx * moms), (rel // moms) % nx, rel % moms
        oy, ox, om = lax.rem(iy + ry, ny), lax.rem(ix + rx, nx), lax.rem(me + rm, moms)
        return om, (oy * nz + iz) * nx + ox, (oy * nx + ox) * moms + om

    @pl.loop(1, plane_n)
    def _(rel):
        om, oe, _ = plane_peer(rel)
        greet(om, oe)

    chunks = [(at, min(128, 2 * NN - at)) for at in range(0, 2 * NN, 128)]

    for src, dst in ((gg_ref, gg_t), (gl_ref, gl_t)):
        whole = src[...].astype(F32).reshape(rows * pairs, 2 * NN)
        for c, (at, wide) in enumerate(chunks):
            rows_f[c, :, :wide] = whole[:, at : at + wide]
        for p in range(pairs):
            block = jnp.concatenate(
                [
                    rows_f.at[c][pl.ds(p, rows, stride=pairs), :][:, :wide]
                    for c, (_, wide) in enumerate(chunks)
                ],
                axis=1,
            ).astype(BF)
            dst[p] = block.reshape(dst.shape[1:])
    for pp in range(pp_n):
        gg[pp, pl.ds(pl.multiple_of(me * rows, 16), rows), :] = gg_t[me * pp_n + pp]
        gl[1, pp, pl.ds(me * own_k, own_k), pl.ds(0, own_e), :] = gl_t[me * pp_n + pp]

    pl.semaphore_wait(barrier, 3 * moms - 1 + nz - 1 + plane_n - 1)

    def gg_copy(rel):
        to = lax.rem(me + rel, moms)
        return pltpu.make_async_remote_copy(
            src_ref=gg_t.at[pl.ds(to * pp_n, pp_n)],
            dst_ref=gg.at[:, pl.ds(pl.multiple_of(me * rows, 16), rows), :],
            send_sem=s_gg.at[rel], recv_sem=r_gg.at[me],
            device_id={"mom": to, "en": en}, device_id_type=MESH,
        )

    def gl_copy(slot, rel, target):
        to = lax.rem(me + rel, moms)
        return pltpu.make_async_remote_copy(
            src_ref=gl_t.at[pl.ds(to * pp_n, pp_n)],
            dst_ref=gl.at[slot, :, pl.ds(me * own_k, own_k), pl.ds(0, own_e), :],
            send_sem=s_gl.at[slot, rel], recv_sem=r_gl.at[slot, me],
            device_id={"mom": to, "en": target}, device_id_type=MESH,
        )

    sent = [gg_copy(rel) for rel in range(1, moms)]
    sent += [gl_copy(1, rel, en) for rel in range(1, moms)]
    sent += [gl_copy(2, rel, down) for rel in range(moms)]
    sent += [gl_copy(0, rel, up) for rel in range(moms)]
    for copy in sent:
        copy.start()

    def await_gg():
        for rel in range(1, moms):
            at = lax.rem(me + rel, moms)
            view = gg.at[:, pl.ds(pl.multiple_of(at * rows, 16), rows), :]
            pltpu.make_async_copy(view, view, r_gg.at[at]).wait()

    def await_gl(slot):
        for rel in range(1 if slot == 1 else 0, moms):
            at = lax.rem(me + rel, moms)
            view = gl.at[slot, :, pl.ds(at * own_k, own_k), pl.ds(0, own_e), :]
            pltpu.make_async_copy(view, view, r_gl.at[slot, at]).wait()

    first_part = lax.broadcasted_iota(jnp.int32, (NN, 2 * NN), 1) < NN

    def split(x):
        hi = x.astype(BF)
        return hi, (x - hi.astype(F32)).astype(BF)

    def expand(row, rows_of, cols_of):
        hi, lo = split(row)
        out = jnp.dot(rows_of * hi, cols_of, preferred_element_type=F32)
        return out + jnp.dot(rows_of * lo, cols_of, preferred_element_type=F32)

    atom = (me * pp_n) // NB
    lefts = [
        expand(der_ref[atom, pl.ds(m, 1), :], rs_ref[...], ci_ref[...]) for m in range(3)
    ]
    for pp in range(pp_n):
        pair = me * pp_n + pp
        other = nb_ref[pair // NB, lax.rem(pair, NB)]
        for m in range(3):
            right = expand(der_ref[other, pl.ds(m, 1), :], rt_ref[...], cu_ref[...])
            both = lefts[m] * right
            for half, keep in ((0, first_part), (1, jnp.logical_not(first_part))):
                hi, lo = split(jnp.where(keep, both, 0.0))
                kr_hi[pp, m, NN * half : NN * (half + 1), :] = hi
                kr_lo[pp, m, NN * half : NN * (half + 1), :] = lo

    lane = lax.broadcasted_iota(jnp.int32, (own_e, 128), 1)
    row = lax.broadcasted_iota(jnp.int32, (own_e, 128), 0)
    spot = lax.rem(lane, 32)

    def turn(lo, hi, blocks):
        blocks = blocks % 8
        if blocks >= 4:
            lo, hi, blocks = hi, lo, blocks - 4
        if blocks == 0:
            return lo, hi
        a, b = pltpu.roll(lo, 32 * blocks, 1), pltpu.roll(hi, 32 * blocks, 1)
        keep = lane >= 32 * blocks
        return jnp.where(keep, a, b), jnp.where(keep, b, a)

    def slide(vector):
        lo = jnp.broadcast_to(vector[:, :128], (own_e, 128))
        hi = jnp.broadcast_to(vector[:, 128:], (own_e, 128))
        a = pltpu.roll(lo, 0, 1, stride=1, stride_axis=0)
        b = pltpu.roll(hi, 0, 1, stride=1, stride_axis=0)
        keep = lane >= row
        return jnp.where(keep, a, b), jnp.where(keep, b, a)

    span = 32 * momenta
    has_low = (en > 0).astype(F32)
    has_up = (en < ens - 1).astype(F32)
    zeros = jnp.zeros((1, span), F32)
    for pp in range(pp_n):
        for m in range(3):
            vec = coef_ref[me * pp_n + pp, pl.ds(m, 1), :]
            part_of = [vec[:, span * i : span * (i + 1)] for i in range(5)]
            combos = (
                (part_of[0] * has_low, zeros),
                (part_of[1], part_of[2]),
                (part_of[3] * has_up, part_of[4] * has_up),
            )
            for slot, (plus, minus) in enumerate(combos):
                plus, minus = slide(plus), slide(minus)
                lo = jnp.where(spot >= row, plus[0], minus[0])
                hi = jnp.where(spot >= row, plus[1], minus[1])
                for k in range(0, momenta, 2):
                    even, odd = turn(lo, hi, k), turn(lo, hi, k + 1)
                    at = m * all_rows + k * own_e
                    for side in range(2):
                        both = jnp.concatenate([even[side], odd[side]], axis=0)
                        toe[slot, pp, at : at + 2 * own_e, 128 * side : 128 * (side + 1)] = (
                            both.astype(BF)
                        )

    nt = (((1,), (1,)), ((), ()))
    await_gg()
    for pp in range(pp_n):
        swapped = jnp.dot(gg[pp], swap_ref[...], preferred_element_type=F32).astype(BF)
        for m in range(3):
            w = lax.dot_general(swapped, kr_hi[pp, m], nt, preferred_element_type=F32)
            w = w + lax.dot_general(swapped, kr_lo[pp, m], nt, preferred_element_type=F32)
            wgt[pp, m] = w.astype(BF)

    def window(slot, pp):
        g = gl[slot, pp].reshape(span, 2 * NN)
        for m in range(3):
            t = toe[slot, pp, m * all_rows : (m + 1) * all_rows, :]
            h = jnp.dot(t, g, preferred_element_type=F32)
            if slot == 1:
                acc[pp, m] = h
            else:
                acc[pp, m] += h

    def pair_sums(slot, pp, m):
        g = gl[slot, pp].reshape(span, 2 * NN)
        z = lax.dot_general(wgt[pp, m], g, nt, preferred_element_type=F32)
        total = None
        for k in range(4):
            a = z[own_e * k : own_e * (k + 1)]
            b = z[own_e * (k + 4) : own_e * (k + 5)]
            lo, hi = turn(a[:, :128] + b[:, 128:], a[:, 128:] + b[:, :128], 8 - k)
            total = (lo, hi) if total is None else (total[0] + lo, total[1] + hi)
        return total

    step = lax.broadcasted_iota(jnp.int32, (8, 128), 0)

    def diagonals(a, b):
        total = None
        for at in range(0, own_e, 8):
            x = pltpu.roll(a[at : at + 8], (127 - at) % 128, 1)
            x = x + pltpu.roll(b[at : at + 8], (127 + own_e - at) % 128, 1)
            total = x if total is None else total + x
        for bit in (1, 2, 4):
            total = jnp.where(step & bit != 0, pltpu.roll(total, 128 - bit, 1), total)
        return total

    await_gl(1)
    own_sums = {(pp, m): pair_sums(1, pp, m) for pp in range(pp_n) for m in range(3)}
    await_gl(2)
    lines = []
    scale = 1.0 / (NO * np.sqrt(np.float32(momenta * ens * own_e)))
    for pp in range(pp_n):
        for m in range(3):
            above = pair_sums(2, pp, m)
            line = []
            for side in range(2):
                a = jnp.where(spot > row, own_sums[pp, m][side], 0.0)
                b = jnp.where(spot <= row, above[side] * has_up, 0.0)
                line.append(jnp.sum(diagonals(a, b), axis=0, keepdims=True) * scale)
            lines.append(jnp.concatenate(line, axis=1))
    lines.append(jnp.zeros((8 - len(lines), span), F32))
    part[...] = jnp.concatenate(lines, axis=0)
    got_z[iz] = part[...]

    def z_copy(rel):
        to = lax.rem(iz + rel, nz)
        return pltpu.make_async_remote_copy(
            src_ref=part, dst_ref=got_z.at[iz],
            send_sem=s_z.at[rel], recv_sem=r_z.at[iz],
            device_id={"mom": me, "en": (iy * nz + to) * nx + ix}, device_id_type=MESH,
        )

    z_sent = [z_copy(rel) for rel in range(1, nz)]
    for copy in z_sent:
        copy.start()

    for pp in range(pp_n):
        window(1, pp)
        window(2, pp)
    await_gl(0)
    for pp in range(pp_n):
        window(0, pp)
        se = None
        for m in range(3):
            hi, lo = split(acc[pp, m])
            for x, y in ((hi, kr_hi), (lo, kr_hi), (hi, kr_lo)):
                term = jnp.dot(x, y[pp, m], preferred_element_type=F32)
                se = term if se is None else se + term
        se_t[pp] = se.astype(BF)
        se_r[me * pp_n + pp] = se_t[pp, pl.ds(pl.multiple_of(me * rows, 16), rows), :]

    def se_copy(rel):
        to = lax.rem(me + rel, moms)
        return pltpu.make_async_remote_copy(
            src_ref=se_t.at[:, pl.ds(pl.multiple_of(to * rows, 16), rows), :],
            dst_ref=se_r.at[pl.ds(me * pp_n, pp_n)],
            send_sem=s_se.at[rel], recv_sem=r_se.at[me],
            device_id={"mom": to, "en": en}, device_id_type=MESH,
        )

    se_sent = [se_copy(rel) for rel in range(1, moms)]
    for copy in se_sent:
        copy.start()

    for rel in range(1, nz):
        at = lax.rem(iz + rel, nz)
        pltpu.make_async_copy(part, got_z.at[at], r_z.at[at]).wait()
    total = got_z[0]
    for z in range(1, nz):
        total = total + got_z[z]
    plane[0] = total[:, :128]
    plane[1] = total[:, 128:]
    mine = (iy * nx + ix) * moms + me
    got_p[mine] = plane[me // 2]

    def p_copy(rel):
        om, oe, _ = plane_peer(rel)
        return pltpu.make_async_remote_copy(
            src_ref=plane.at[om // 2], dst_ref=got_p.at[mine],
            send_sem=s_p.at[rel], recv_sem=r_p.at[mine],
            device_id={"mom": om, "en": oe}, device_id_type=MESH,
        )

    @pl.loop(1, plane_n)
    def _(rel):
        p_copy(rel).start()

    for rel in range(1, moms):
        at = lax.rem(me + rel, moms)
        view = se_r.at[pl.ds(at * pp_n, pp_n)]
        pltpu.make_async_copy(view, view, r_se.at[at]).wait()
    for p in range(pairs):
        block = se_r[p].astype(F32)
        block = jnp.concatenate([block, jnp.zeros((rows, 384 - 2 * NN), F32)], axis=1)
        for c, (at, _) in enumerate(chunks):
            rows_f.at[c][pl.ds(p, rows, stride=pairs), :] = block[:, at : at + 128]
    whole = jnp.concatenate([rows_f[c, :, :wide] for c, (_, wide) in enumerate(chunks)], axis=1)
    se_ref[...] = whole.reshape(own_k, own_e, pairs, 2 * NN).astype(BF)

    @pl.loop(1, plane_n)
    def _(rel):
        _, _, slot = plane_peer(rel)
        pltpu.make_async_copy(got_p.at[slot], got_p.at[slot], r_p.at[slot]).wait()

    odd = lax.rem(me, 2) == 1
    for a in range(moms):
        total = got_p[a]
        for i in range(1, ny * nx):
            total = total + got_p[i * moms + a]
        pol_ref[a] = jnp.where(odd, pltpu.roll(total, 64, 1), total)

    for copy in sent + z_sent + se_sent:
        copy.wait_send()

    @pl.loop(1, plane_n)
    def _(rel):
        p_copy(rel).wait_send()


def body(green_less, green_greater, derivative, neighbours, phonon):
    own_k, own_e, pairs, width = green_less.shape
    momenta, window = phonon.shape[1], phonon.shape[2]
    moms, ens = lax.axis_size("mom"), lax.axis_size("en")
    nx = 2
    nz = min(8, ens // nx)
    ny = ens // (nz * nx)
    dims = (moms, ens, ny, nz, nx, own_k, own_e, pairs, momenta)
    pp_n = pairs // moms
    span = 32 * momenta
    rs, rt, ci, cu, swap, place = (jnp.asarray(t, BF) for t in tables(momenta, window))
    coef = jnp.einsum(
        "rmp,rl->pml", phonon.reshape(2 * momenta * window, 3, pairs), place,
        preferred_element_type=F32,
    )
    vm = pl.BlockSpec(memory_space=pltpu.VMEM)
    rows = own_k * own_e
    all_rows = momenta * own_e
    dma = pltpu.SemaphoreType.DMA
    plane_n = ny * nx * moms
    self_energy, pol = pl.pallas_call(
        functools.partial(kernel, dims),
        out_shape=(
            jax.ShapeDtypeStruct((own_k, own_e, pairs, width), BF),
            jax.ShapeDtypeStruct((moms, 8, 128), F32),
        ),
        in_specs=[vm, vm, vm, pl.BlockSpec(memory_space=pltpu.SMEM)] + [vm] * 6,
        out_specs=(vm, vm),
        scratch_shapes=[
            pltpu.VMEM((3, rows * pairs, 128), F32),
            pltpu.VMEM((pairs, own_k, own_e, width), BF),
            pltpu.VMEM((pairs, rows, width), BF),
            pltpu.VMEM((3, pp_n, momenta, 32, width), BF),
            pltpu.VMEM((pp_n, all_rows, width), BF),
            pltpu.VMEM((3, pp_n, 3 * all_rows, span), BF),
            pltpu.VMEM((pp_n, 3, width, width), BF),
            pltpu.VMEM((pp_n, 3, width, width), BF),
            pltpu.VMEM((pp_n, 3, all_rows, width), BF),
            pltpu.VMEM((pp_n, 3, all_rows, width), F32),
            pltpu.VMEM((pp_n, all_rows, width), BF),
            pltpu.VMEM((pairs, rows, width), BF),
            pltpu.VMEM((8, span), F32),
            pltpu.VMEM((nz, 8, span), F32),
            pltpu.VMEM((2, 8, 128), F32),
            pltpu.VMEM((plane_n, 8, 128), F32),
            dma((moms,)), dma((moms,)), dma((3, moms)), dma((3, moms)),
            dma((moms,)), dma((moms,)), dma((nz,)), dma((nz,)), dma((plane_n,)), dma((plane_n,)),
        ],
        compiler_params=pltpu.CompilerParams(collective_id=0, has_side_effects=True),
    )(green_less, green_greater, derivative, neighbours, coef, rs, rt, ci, cu, swap)
    pol = pol[:, : 3 * pp_n, :64].reshape(moms, pp_n, 3, momenta // moms, 32)[..., :window]
    pol = pol.transpose(3, 4, 2, 0, 1).reshape(momenta // moms, window, 3, pairs)
    return self_energy, pol


def solution(mesh):
    return jax.shard_map(
        body,
        mesh=mesh,
        in_specs=(P("mom", "en", None, None), P("mom", "en", None, None), P(), P(), P()),
        out_specs=(P("mom", "en", None, None), P("mom", None, None, None)),
        check_vma=False,
    )
```

profile of v0, /device:TPU:1, one launch (start us, length us, event | category | flops | bytes accessed | tf_op | source)
XLA Modules:
  0.0 49.4 jit_solution(15696427076495041919)
XLA Ops:
  0.6 1.3 %copy.22.der_ref = f32[2,3,144]{2,1,0:T(4,128)} copy(f32[2,3,144]{2,0,1:T(2,128)} %param.13) | data formatting | bytes 6912 | tf_op args[2]
  1.9 0.9 %copy.20 = bf16[2,8,24,3,8]{2,1,0,4,3:T(8,128)(2,1)S(1)} copy(bf16[2,8,24,3,8]{2,4,3,1,0:T(8,128)(2,1)} %param.15) | data formatting | bytes 36864 | tf_op args[4]
  2.8 0.1 reshape.16
  3.0 1.4 %convolution_bitcast_fusion = f32[1280,3,8]{0,2,1:T(8,128)S(1)} fusion(bf16[384,1280]{1,0:T(8,128)(2,1)} %constant.17.clone, bf16[384,24]{0,1:T(8,128)(2,1)S(1)} %reshape.16), kind=kOutput, calls=%fused_computation | convolution fusion | flops 23592960 | bytes 1124352
  4.4 0.7 %copy.26 = f32[1280,3,8]{0,1,2:T(4,128)} copy(f32[1280,3,8]{0,2,1:T(8,128)S(1)} %convolution_bitcast_fusion) | data formatting | bytes 245760 | tf_op jit(solution)/shard_map/rmp,rl->pml/dot_general | solution.py:390
  5.2 41.1 %shard_map.122 = (bf16[2,24,8,288]{3,2,1,0:T(8,128)(2,1)}, f32[4,8,128]{2,1,0:T(8,128)}) custom-call(bf16[2,24,8,288]{3,2,1,0:T(8,128)(2,1)} %gl_ref.1, bf16[2,24,8,288]{3,2,1,0:T(8,128)(2,1)} %gg_ref.1, f32[2,3,144]{2,1,0:T(4,128)} %copy.22.der_ref, s32[2,4]{1,0:T(2,128)} %nb_ref.1, f32[8,3,1280]{2,1,0:T(4,128)} %bitcast.17, ...), custom_call_target="tpu_custom_call" | custom-call | tf_op jit(solution)/shard_map/pallas_call | solution.py:399
  46.3 0.7 %copy.23 = f32[4,6,64]{2,0,1:T(4,128)S(1)} copy(f32[4,6,64]{2,1,0:T(8,128)} %bitcast.19) | data formatting | bytes 12288 | tf_op jit(solution)/shard_map/slice | solution.py:429
  47.0 0.1 reshape.14
  47.1 0.6 %copy.24 = f32[2,24,3,4,2]{1,4,3,2,0:T(2,128)} copy(f32[2,24,3,4,2]{1,0,3,2,4:T(2,128)S(1)} %slice_bitcast_fusion) | data formatting | bytes 9216 | tf_op jit(solution)/shard_map/transpose | solution.py:430
  47.7 1.7 %copy.28 = bf16[2,24,8,288]{3,2,1,0:T(8,128)(2,1)} copy(bf16[2,24,8,288]{3,2,1,0:T(8,128)(2,1)} %get-tuple-element.8) | data formatting | bytes 442368
  (1 shorter events, 0.0 us)
where the time goes:
time: 49.7 us; the launch traced here: 49.4 us
  Pallas kernels  41.1 us (83%)
  local copies, waits for them, and re-layouts  6.23 us (13%)
  matrix products  1.44 us (3%)
  between operations  0.66 us (1%)
    pallas_call x1, Pallas kernels, body(): pl.pallas_call(functools.partial(kernel, dims), out_shape=(jax.ShapeDtype...  41.1 us
    unnamed x4, local copies, waits for them, and re-layouts  4.05 us
    unnamed x1, matrix products  1.44 us

commit v1 on v0

v1 whole, which is shorter than its diff:
```python
import functools

import jax
import jax.numpy as jnp
import numpy as np
from jax import lax
from jax.experimental import pallas as pl
from jax.experimental.pallas import tpu as pltpu
from jax.sharding import PartitionSpec as P

NO = 12
NB = 4
NN = NO * NO
MAIN = 256
TAIL = 2 * NN - MAIN
WIDE = MAIN + 128
MESH = pl.DeviceIdType.MESH
BF = jnp.bfloat16
F32 = jnp.float32
NT = (((1,), (1,)), ((), ()))


def tables(pp_n):
    r = np.arange(NN)
    col = np.arange(2 * NN)
    sub = col % NN
    rows_s = (r[None, :] % NO == r[:, None] // NO).astype(np.float32)
    rows_t = (r[None, :] % NO == r[:, None] % NO).astype(np.float32)
    cols_i = np.zeros((NN, WIDE), np.float32)
    cols_u = np.zeros((NN, WIDE), np.float32)
    cols_i[:, : 2 * NN] = r[:, None] // NO == sub[None, :] // NO
    cols_u[:, : 2 * NN] = r[:, None] // NO == sub[None, :] % NO
    swap = np.zeros((pp_n, WIDE, WIDE), np.float32)
    flipped = (col // NN) * NN + (sub % NO) * NO + sub // NO
    for pp in range(pp_n):
        at = np.where(col < MAIN, col, col + TAIL * pp)
        swap[pp, at[flipped], at] = np.where(col < NN, 1.0, -1.0)
    return rows_s, rows_t, cols_i, cols_u, swap


def split(x):
    hi = x.astype(BF)
    return hi, (x - hi.astype(F32)).astype(BF)


def kernel(
    dims,
    gl_ref, gg_ref, der_ref, nb_ref, ph_ref, rs_ref, rt_ref, ci_ref, cu_ref, swap_ref,
    se_r, pol_ref,
    rows_f, gl_t, gg_t, gl, gg, coef, toe, kr_hi, kr_lo, wgt, acc, se_t, part, got_z, plane, got_p,
    s_gg, r_gg, s_gl, r_gl, s_se, r_se, s_z, r_z, s_p, r_p,
):
    moms, ens, ny, nz, nx, own_k, own_e, pairs, momenta, window_n = dims
    pp_n = pairs // moms
    rows = own_k * own_e
    all_rows = momenta * own_e
    span = 32 * momenta
    cols = MAIN * pp_n + 128
    me = lax.axis_index("mom")
    en = lax.axis_index("en")
    iy, iz, ix = en // (nz * nx), (en // nx) % nz, en % nx
    up, down = lax.rem(en + 1, ens), lax.rem(en + ens - 1, ens)

    gl[:, :, own_e:, :] = jnp.zeros((3, momenta, 32 - own_e, cols), BF)

    barrier = pltpu.get_barrier_semaphore()

    def greet(mom_at, en_at):
        pl.semaphore_signal(
            barrier, inc=1, device_id={"mom": mom_at, "en": en_at}, device_id_type=MESH
        )

    for rel in range(1, moms):
        greet(lax.rem(me + rel, moms), en)
    for rel in range(moms):
        greet(lax.rem(me + rel, moms), up)
        greet(lax.rem(me + rel, moms), down)
    for rel in range(1, nz):
        greet(me, (iy * nz + lax.rem(iz + rel, nz)) * nx + ix)
    plane_n = ny * nx * moms

    def plane_peer(rel):
        ry, rx, rm = rel // (nx * moms), (rel // moms) % nx, rel % moms
        oy, ox, om = lax.rem(iy + ry, ny), lax.rem(ix + rx, nx), lax.rem(me + rm, moms)
        return om, (oy * nz + iz) * nx + ox, (oy * nx + ox) * moms + om

    @pl.loop(1, plane_n)
    def _(rel):
        om, oe, _ = plane_peer(rel)
        greet(om, oe)

    tail_lane = lax.broadcasted_iota(jnp.int32, (rows, 128), 1)

    def by_pair(src, dst):
        whole = src[...].astype(F32).reshape(rows * pairs, 2 * NN)
        rows_f[0] = whole[:, :128]
        rows_f[1] = whole[:, 128:MAIN]
        rows_f[2, :, :TAIL] = whole[:, MAIN:]
        for a in range(moms):
            tail = jnp.zeros((rows, 128), F32)
            parts = []
            for pp in range(pp_n):
                x = [rows_f.at[c][pl.ds(a * pp_n + pp, rows, stride=pairs), :] for c in range(3)]
                parts += x[:2]
                last = pltpu.roll(x[2], TAIL * pp, 1) if pp else x[2]
                keep = (tail_lane >= TAIL * pp) & (tail_lane < TAIL * (pp + 1))
                tail = jnp.where(keep, last, tail)
            block = jnp.concatenate(parts + [tail], axis=1).astype(BF)
            dst[a] = block.reshape(dst.shape[1:])

    by_pair(gg_ref, gg_t)
    pl.semaphore_wait(barrier, 3 * moms - 1 + nz - 1 + plane_n - 1)

    def gg_copy(rel):
        to = lax.rem(me + rel, moms)
        return pltpu.make_async_remote_copy(
            src_ref=gg_t.at[to],
            dst_ref=gg.at[pl.ds(pl.multiple_of(me * rows, 16), rows), :],
            send_sem=s_gg.at[rel], recv_sem=r_gg.at[me],
            device_id={"mom": to, "en": en}, device_id_type=MESH,
        )

    def gl_copy(slot, rel, target):
        to = lax.rem(me + rel, moms)
        return pltpu.make_async_remote_copy(
            src_ref=gl_t.at[to],
            dst_ref=gl.at[slot, pl.ds(me * own_k, own_k), pl.ds(0, own_e), :],
            send_sem=s_gl.at[slot, rel], recv_sem=r_gl.at[slot, me],
            device_id={"mom": to, "en": target}, device_id_type=MESH,
        )

    sent = [gg_copy(rel) for rel in range(1, moms)]
    for copy in sent:
        copy.start()
    by_pair(gl_ref, gl_t)
    more = [gl_copy(1, rel, en) for rel in range(1, moms)]
    more += [gl_copy(2, rel, down) for rel in range(moms)]
    more += [gl_copy(0, rel, up) for rel in range(moms)]
    for copy in more:
        copy.start()
    sent += more
    gg[pl.ds(pl.multiple_of(me * rows, 16), rows), :] = gg_t[me]
    gl[1, pl.ds(me * own_k, own_k), pl.ds(0, own_e), :] = gl_t[me]

    def await_gg():
        for rel in range(1, moms):
            at = lax.rem(me + rel, moms)
            view = gg.at[pl.ds(pl.multiple_of(at * rows, 16), rows), :]
            pltpu.make_async_copy(view, view, r_gg.at[at]).wait()

    def await_gl(slot):
        for rel in range(1 if slot == 1 else 0, moms):
            at = lax.rem(me + rel, moms)
            view = gl.at[slot, pl.ds(at * own_k, own_k), pl.ds(0, own_e), :]
            pltpu.make_async_copy(view, view, r_gl.at[slot, at]).wait()

    first_part = lax.broadcasted_iota(jnp.int32, (NN, WIDE), 1) < NN

    def expand(row, rows_of, cols_of):
        hi, lo = split(row)
        out = jnp.dot(rows_of * hi, cols_of, preferred_element_type=F32)
        return out + jnp.dot(rows_of * lo, cols_of, preferred_element_type=F32)

    atom = (me * pp_n) // NB

    def block_of(m, index):
        found = der_ref[m, 0:1, :]
        for i in range(1, der_ref.shape[1]):
            found = jnp.where(index == i, der_ref[m, i : i + 1, :], found)
        return found

    lefts = [expand(block_of(m, atom), rs_ref[...], ci_ref[...]) for m in range(3)]
    cut = MAIN - NN
    for pp in range(pp_n):
        pair = me * pp_n + pp
        other = nb_ref[pair // NB, lax.rem(pair, NB)]
        for m in range(3):
            right = expand(block_of(m, other), rt_ref[...], cu_ref[...])
            both = lefts[m] * right
            top = jnp.where(first_part, both, 0.0)
            low = jnp.where(first_part, 0.0, both)
            if pp:
                low = jnp.concatenate(
                    [low[:, :MAIN], pltpu.roll(low[:, MAIN:], TAIL * pp, 1)], axis=1
                )
            for dst, a, b in zip((kr_hi, kr_lo), split(top), split(low)):
                dst[pp, m, :NN, :] = a
                dst[pp, m, NN:MAIN, :] = b[:cut]
                dst[pp, m, MAIN:, :] = jnp.zeros((128, WIDE), BF)
                dst[pp, m, MAIN + TAIL * pp : MAIN + TAIL * (pp + 1), :] = b[cut:]

    lane = lax.broadcasted_iota(jnp.int32, (own_e, 128), 1)
    row = lax.broadcasted_iota(jnp.int32, (own_e, 128), 0)
    spot = lax.rem(lane, 32)

    def ring(lo, hi, n):
        n = n % span
        if n >= 128:
            lo, hi, n = hi, lo, n - 128
        if n == 0:
            return lo, hi
        a, b = pltpu.roll(lo, n, 1), pltpu.roll(hi, n, 1)
        keep = lane >= n
        return jnp.where(keep, a, b), jnp.where(keep, b, a)

    def slide(at, index):
        lo, hi = (coef.at[at, side][pl.ds(index, own_e, stride=0), :] for side in range(2))
        a = pltpu.roll(lo, 0, 1, stride=1, stride_axis=0)
        b = pltpu.roll(hi, 0, 1, stride=1, stride_axis=0)
        keep = lane >= row
        return jnp.where(keep, a, b), jnp.where(keep, b, a)

    lines = 3 * pairs
    w_at = lax.broadcasted_iota(jnp.int32, (window_n, 128), 0)
    l_at = lax.broadcasted_iota(jnp.int32, (window_n, 128), 1)
    places = (l_at == window_n - 1 - w_at, l_at == w_at)
    for s in range(2):
        flat = ph_ref[s].reshape(momenta * lines, window_n)
        spread = jnp.dot(
            flat, jnp.where(places[s], 1.0, 0.0).astype(BF), preferred_element_type=F32
        )
        sides = [None, None]
        for q in range(momenta):
            block = (momenta - q) % momenta
            x = spread[lines * q : lines * (q + 1)]
            if block % 4:
                x = pltpu.roll(x, 32 * (block % 4), 1)
            sides[block // 4] = x if sides[block // 4] is None else sides[block // 4] + x
        for at, n in ((2 * s, (0, 1)[s]), (2 * s + 1, (span - window_n, span + 1 - window_n)[s])):
            lo, hi = ring(sides[0], sides[1], n)
            coef[at, 0] = lo
            coef[at, 1] = hi

    has_low = (en > 0).astype(F32)
    has_up = (en < ens - 1).astype(F32)
    for pp in range(pp_n):
        for m in range(3):
            index = m * pairs + me * pp_n + pp
            absorb, absorb_own = slide(0, index), slide(1, index)
            emit_own, emit = slide(2, index), slide(3, index)
            for slot in range(3):
                pick = []
                for side in range(2):
                    if slot == 0:
                        x = jnp.where(spot >= row, absorb[side] * has_low, 0.0)
                    elif slot == 1:
                        x = jnp.where(spot >= row, emit_own[side], absorb_own[side])
                    else:
                        x = jnp.where(spot <= row, emit[side] * has_up, 0.0)
                    pick.append(x)
                for k in range(0, momenta, 2):
                    even, odd = ring(*pick, 32 * k), ring(*pick, 32 * (k + 1))
                    at = m * all_rows + k * own_e
                    for side in range(2):
                        both = jnp.concatenate([even[side], odd[side]], axis=0)
                        toe[slot, pp, at : at + 2 * own_e, 128 * side : 128 * (side + 1)] = (
                            both.astype(BF)
                        )

    def of_pair(block, pp):
        return jnp.concatenate(
            [block[:, MAIN * pp : MAIN * (pp + 1)], block[:, MAIN * pp_n :]], axis=1
        )

    await_gg()
    for pp in range(pp_n):
        swapped = jnp.dot(
            of_pair(gg[...], pp), swap_ref[pp], preferred_element_type=F32
        ).astype(BF)
        for m in range(3):
            w = lax.dot_general(swapped, kr_hi[pp, m], NT, preferred_element_type=F32)
            w = w + lax.dot_general(swapped, kr_lo[pp, m], NT, preferred_element_type=F32)
            wgt[pp, m] = w.astype(BF)

    def window(slot, pp):
        g = of_pair(gl[slot].reshape(span, cols), pp)
        for m in range(3):
            t = toe[slot, pp, m * all_rows : (m + 1) * all_rows, :]
            h = jnp.dot(t, g, preferred_element_type=F32)
            if slot == 1:
                acc[pp, m] = h
            else:
                acc[pp, m] += h

    def pair_sums(slot, pp, m):
        g = of_pair(gl[slot].reshape(span, cols), pp)
        z = lax.dot_general(wgt[pp, m], g, NT, preferred_element_type=F32)
        total = None
        for k in range(4):
            a = z[own_e * k : own_e * (k + 1)]
            b = z[own_e * (k + 4) : own_e * (k + 5)]
            lo, hi = ring(a[:, :128] + b[:, 128:], a[:, 128:] + b[:, :128], span - 32 * k)
            total = (lo, hi) if total is None else (total[0] + lo, total[1] + hi)
        return total

    step = lax.broadcasted_iota(jnp.int32, (8, 128), 0)

    def diagonals(a, b):
        total = None
        for at in range(0, own_e, 8):
            x = pltpu.roll(a[at : at + 8], (127 - at) % 128, 1)
            x = x + pltpu.roll(b[at : at + 8], (127 + own_e - at) % 128, 1)
            total = x if total is None else total + x
        for bit in (1, 2, 4):
            total = jnp.where(step & bit != 0, pltpu.roll(total, 128 - bit, 1), total)
        return total

    await_gl(1)
    own_sums = {(pp, m): pair_sums(1, pp, m) for pp in range(pp_n) for m in range(3)}
    await_gl(2)
    found = []
    scale = 1.0 / (NO * np.sqrt(np.float32(momenta * ens * own_e)))
    for pp in range(pp_n):
        for m in range(3):
            above = pair_sums(2, pp, m)
            line = []
            for side in range(2):
                a = jnp.where(spot > row, own_sums[pp, m][side], 0.0)
                b = jnp.where(spot <= row, above[side] * has_up, 0.0)
                line.append(jnp.sum(diagonals(a, b), axis=0, keepdims=True) * scale)
            found.append(jnp.concatenate(line, axis=1))
    found.append(jnp.zeros((8 - len(found), span), F32))
    part[...] = jnp.concatenate(found, axis=0)
    got_z[iz] = part[...]

    def z_copy(rel):
        to = lax.rem(iz + rel, nz)
        return pltpu.make_async_remote_copy(
            src_ref=part, dst_ref=got_z.at[iz],
            send_sem=s_z.at[rel], recv_sem=r_z.at[iz],
            device_id={"mom": me, "en": (iy * nz + to) * nx + ix}, device_id_type=MESH,
        )

    z_sent = [z_copy(rel) for rel in range(1, nz)]
    for copy in z_sent:
        copy.start()

    for pp in range(pp_n):
        window(1, pp)
        window(2, pp)
    await_gl(0)
    tail = None
    for pp in range(pp_n):
        window(0, pp)
        se = None
        for m in range(3):
            hi, lo = split(acc[pp, m])
            for x, y in ((hi, kr_hi), (lo, kr_hi), (hi, kr_lo)):
                term = jnp.dot(x, y[pp, m], preferred_element_type=F32)
                se = term if se is None else se + term
        se_t[:, MAIN * pp : MAIN * (pp + 1)] = se[:, :MAIN].astype(BF)
        tail = se[:, MAIN:] if tail is None else tail + se[:, MAIN:]
    se_t[:, MAIN * pp_n :] = tail.astype(BF)

    def se_copy(rel):
        to = lax.rem(me + rel, moms)
        return pltpu.make_async_remote_copy(
            src_ref=se_t.at[pl.ds(pl.multiple_of(to * rows, 16), rows), :],
            dst_ref=se_r.at[me],
            send_sem=s_se.at[rel], recv_sem=r_se.at[me],
            device_id={"mom": to, "en": en}, device_id_type=MESH,
        )

    se_sent = [se_copy(rel) for rel in range(1, moms)]
    for copy in se_sent:
        copy.start()
    se_r[me] = se_t[pl.ds(pl.multiple_of(me * rows, 16), rows), :]

    for rel in range(1, nz):
        at = lax.rem(iz + rel, nz)
        pltpu.make_async_copy(part, got_z.at[at], r_z.at[at]).wait()
    total = got_z[0]
    for z in range(1, nz):
        total = total + got_z[z]
    plane[0] = total[:, :128]
    plane[1] = total[:, 128:]
    mine = (iy * nx + ix) * moms + me
    got_p[mine] = plane[me // 2]

    def p_copy(rel):
        om, oe, _ = plane_peer(rel)
        return pltpu.make_async_remote_copy(
            src_ref=plane.at[om // 2], dst_ref=got_p.at[mine],
            send_sem=s_p.at[rel], recv_sem=r_p.at[mine],
            device_id={"mom": om, "en": oe}, device_id_type=MESH,
        )

    @pl.loop(1, plane_n)
    def _(rel):
        p_copy(rel).start()

    for copy in sent + z_sent + se_sent:
        copy.wait_send()

    for rel in range(1, moms):
        at = lax.rem(me + rel, moms)
        pltpu.make_async_copy(se_r.at[at], se_r.at[at], r_se.at[at]).wait()

    @pl.loop(1, plane_n)
    def _(rel):
        _, _, slot = plane_peer(rel)
        pltpu.make_async_copy(got_p.at[slot], got_p.at[slot], r_p.at[slot]).wait()

    odd = lax.rem(me, 2) == 1
    for a in range(moms):
        total = got_p[a]
        for i in range(1, ny * nx):
            total = total + got_p[i * moms + a]
        pol_ref[a] = jnp.where(odd, pltpu.roll(total, 64, 1), total)

    @pl.loop(1, plane_n)
    def _(rel):
        p_copy(rel).wait_send()


def finish(se_ref, pol_ref, out_ref, pol_out, rows_f):
    own_k, own_e, pairs, _ = out_ref.shape
    moms, rows, _ = se_ref.shape
    pp_n = pairs // moms
    for a in range(moms):
        block = se_ref[a].astype(F32)
        tail = block[:, MAIN * pp_n :]
        for pp in range(pp_n):
            at = pl.ds(a * pp_n + pp, rows, stride=pairs)
            rows_f.at[0][at, :] = block[:, MAIN * pp : MAIN * pp + 128]
            rows_f.at[1][at, :] = block[:, MAIN * pp + 128 : MAIN * (pp + 1)]
            rows_f.at[2][at, :] = pltpu.roll(tail, 128 - TAIL * pp, 1) if pp else tail
    whole = jnp.concatenate([rows_f[0], rows_f[1], rows_f[2, :, :TAIL]], axis=1)
    out_ref[...] = whole.reshape(own_k, own_e, pairs, 2 * NN).astype(BF)
    own_q, _, _, window_n = pol_out.shape
    for a in range(moms):
        total = pol_ref[a]
        for q in range(own_q):
            x = pltpu.roll(total, 128 - 32 * q, 1) if q else total
            for pp in range(pp_n):
                for m in range(3):
                    line = pp * 3 + m
                    pol_out[q, m, a * pp_n + pp, :] = x[line, :window_n]


def body(green_less, green_greater, derivative, neighbours, phonon):
    own_k, own_e, pairs, width = green_less.shape
    momenta, window_n = phonon.shape[1], phonon.shape[2]
    moms, ens = lax.axis_size("mom"), lax.axis_size("en")
    nx = 2
    nz = min(8, ens // nx)
    ny = ens // (nz * nx)
    dims = (moms, ens, ny, nz, nx, own_k, own_e, pairs, momenta, window_n)
    pp_n = pairs // moms
    span = 32 * momenta
    constants = [jnp.asarray(t, BF) for t in tables(pp_n)]
    vm = pl.BlockSpec(memory_space=pltpu.VMEM)
    rows = own_k * own_e
    all_rows = momenta * own_e
    cols = MAIN * pp_n + 128
    dma = pltpu.SemaphoreType.DMA
    plane_n = ny * nx * moms
    blocks, sums = pl.pallas_call(
        functools.partial(kernel, dims),
        out_shape=(
            jax.ShapeDtypeStruct((moms, rows, cols), BF),
            jax.ShapeDtypeStruct((moms, 8, 128), F32),
        ),
        in_specs=[vm, vm, vm, pl.BlockSpec(memory_space=pltpu.SMEM)] + [vm] * 6,
        out_specs=(vm, vm),
        scratch_shapes=[
            pltpu.VMEM((3, rows * pairs, 128), F32),
            pltpu.VMEM((moms, own_k, own_e, cols), BF),
            pltpu.VMEM((moms, rows, cols), BF),
            pltpu.VMEM((3, momenta, 32, cols), BF),
            pltpu.VMEM((all_rows, cols), BF),
            pltpu.VMEM((4, 2, 3 * pairs, 128), F32),
            pltpu.VMEM((3, pp_n, 3 * all_rows, span), BF),
            pltpu.VMEM((pp_n, 3, WIDE, WIDE), BF),
            pltpu.VMEM((pp_n, 3, WIDE, WIDE), BF),
            pltpu.VMEM((pp_n, 3, all_rows, WIDE), BF),
            pltpu.VMEM((pp_n, 3, all_rows, WIDE), F32),
            pltpu.VMEM((all_rows, cols), BF),
            pltpu.VMEM((8, span), F32),
            pltpu.VMEM((nz, 8, span), F32),
            pltpu.VMEM((2, 8, 128), F32),
            pltpu.VMEM((plane_n, 8, 128), F32),
            dma((moms,)), dma((moms,)), dma((3, moms)), dma((3, moms)),
            dma((moms,)), dma((moms,)), dma((nz,)), dma((nz,)), dma((plane_n,)), dma((plane_n,)),
        ],
        compiler_params=pltpu.CompilerParams(collective_id=0, has_side_effects=True),
    )(
        green_less, green_greater, derivative.transpose(1, 0, 2), neighbours,
        phonon.transpose(0, 1, 3, 4, 2), *constants,
    )
    self_energy, pol = pl.pallas_call(
        finish,
        out_shape=(
            jax.ShapeDtypeStruct((own_k, own_e, pairs, width), BF),
            jax.ShapeDtypeStruct((momenta // moms, 3, pairs, window_n), F32),
        ),
        in_specs=[vm, vm],
        out_specs=(vm, vm),
        scratch_shapes=[pltpu.VMEM((3, rows * pairs, 128), F32)],
    )(blocks, sums)
    return self_energy, pol.transpose(0, 3, 1, 2)


def solution(mesh):
    return jax.shard_map(
        body,
        mesh=mesh,
        in_specs=(P("mom", "en", None, None), P("mom", "en", None, None), P(), P(), P()),
        out_specs=(P("mom", "en", None, None), P("mom", None, None, None)),
        check_vma=False,
    )
```

time: 49.7 us -> 41.8 us (0.84)
  local copies, waits for them, and re-layouts: 6.23 us -> 0 us
  matrix products: 1.44 us -> 0 us
    unnamed x4 -> x0, local copies, waits for them, and re-layouts: 4.05 us -> none
    pallas_call x1, Pallas kernels: 41.1 us -> 39.2 us  [body(): pl.pallas_call(functools.partial(kernel, dims), out_shape=(jax.ShapeDtype...]
    pallas_call x0 -> x1, Pallas kernels: none -> 1.81 us  [body(): pl.pallas_call(finish, out_shape=(jax.ShapeDtypeStruct((own_k, own_e, pai...]
    unnamed x1 -> x0, matrix products: 1.44 us -> none
    dot_general x1 -> x0, local copies, waits for them, and re-layouts: 0.74 us -> none  [body(): jnp.einsum('rmp,rl->pml', phonon.reshape(2 * momenta * window, 3, pairs),...]
    slice x1 -> x0, local copies, waits for them, and re-layouts: 0.72 us -> none  [body(): pol[:, :3 * pp_n, :64].reshape(moms, pp_n, 3, momenta // moms, 32)]
    transpose x2 -> x0, local copies, waits for them, and re-layouts: 0.63 us -> none  [body(): pol.transpose(3, 4, 2, 0, 1).reshape(momenta // moms, window, 3, pairs)]
where the time goes in v1:
time: 41.8 us; the launch traced here: 41.7 us
  Pallas kernels  41 us (98%)
  between operations  0.64 us (2%)
    pallas_call x1, Pallas kernels, body(): pl.pallas_call(functools.partial(kernel, dims), out_shape=(jax.ShapeDtype...  39.2 us
    pallas_call x1, Pallas kernels, body(): pl.pallas_call(finish, out_shape=(jax.ShapeDtypeStruct((own_k, own_e, pai...  1.81 us

profile of v1, /device:TPU:1, one launch (start us, length us, event | category | flops | bytes accessed | tf_op | source)
XLA Modules:
  0.0 41.7 jit_solution(8706399280969820190)
XLA Ops:
  0.6 39.2 %shard_map.113 = (bf16[4,48,640]{2,1,0:T(8,128)(2,1)}, f32[4,8,128]{2,1,0:T(8,128)}) custom-call(bf16[2,24,8,288]{3,2,1,0:T(8,128)(2,1)} %gl_ref.1, bf16[2,24,8,288]{3,2,1,0:T(8,128)(2,1)} %gg_ref.1, f32[3,2,144]{2,1,0:T(2,128)} %bitcast.4, s32[2,4]{1,0:T(2,128)} %nb_ref.1, bf16[2,8,3,8,24]{4,3,2,1,0:T(8,128)(2,1)} %bitcast.3, ...), custom_call_target="tpu_custom_call" | custom-call | tf_op jit(solution)/shard_map/pallas_call | solution.py:458
  39.8 1.8 %shard_map.114 = (bf16[2,24,8,288]{3,2,1,0:T(8,128)(2,1)}, f32[2,3,8,24]{3,2,1,0:T(8,128)}) custom-call(bf16[4,48,640]{2,1,0:T(8,128)(2,1)} %get-tuple-element.6.se_ref, f32[4,8,128]{2,1,0:T(8,128)} %get-tuple-element.7.pol_ref), custom_call_target="tpu_custom_call" | custom-call | tf_op jit(solution)/shard_map/pallas_call | solution.py:491
